TPU v7x, 256 devices: a whole 4x4x8 slice. The times are simulated.
256 devices in a mesh: dp: 8 (over y, core), ctx: 32 (over x, z).
Axes of the slice: x: 4, y: 4, z: 8, core: 2. Of those that a mesh axis runs over, the one named last changes fastest.
Arguments:
- features: bfloat16 [8, 4096, 1536], P('dp', 'ctx'), may hold values from -6 to 6
- short_weight: float32 [7, 1536], replicated, may hold values from -2 to 2
- long_filter: float32 [4096, 512], P('ctx'), may hold values from -4 to 4
- skip_bias: float32 [512], replicated, may hold values from 0.5 to 1.5
- cotangent: bfloat16 [8, 4096, 512], P('dp', 'ctx'), may hold values from -6 to 6
Outputs:
- layer_out: bfloat16 [8, 4096, 512], P('dp', 'ctx')
- grad_features: bfloat16 [8, 4096, 1536], P('dp', 'ctx')
- grad_short: float32 [7, 1536], replicated
- grad_filter: float32 [4096, 512], P('ctx')
- grad_skip: float32 [512], replicated
All inputs are finite; a program needn't handle non-finite values.
Results may differ from a plain program's by a relative error of at most 0.001.
Values may be sent and summed in bfloat16 or wider, within the bound.
A program may use at most 64 MiB of HBM per device.

v0:
```python
import math
import jax
import jax.numpy as jnp
from jax import lax
from jax.sharding import PartitionSpec as P

PRECISE = lax.Precision.HIGHEST


def swapped(value, axis, distance):
    mask = 2**distance
    pairs = [(source, source ^ mask) for source in range(lax.axis_size(axis))]
    return lax.ppermute(value, axis, pairs)


def shifted(value, axis, steps):
    count = lax.axis_size(axis)
    initial, last = (max(0, -steps), min(count, count - steps))
    return lax.ppermute(value, axis, [(source, source + steps) for source in range(initial, last)])


def bit_reverse(index_value, bit_count):
    reversed_value = jnp.zeros_like(index_value)
    for bit_place in range(bit_count):
        digit_now = index_value // 2**bit_place % 2
        reversed_value = reversed_value + digit_now * 2 ** (bit_count - 1 - bit_place)
    return reversed_value


def spectral_table(device, parts_count, tokens):
    bit_count = parts_count.bit_length() - 1
    coarse_freq = 2 * bit_reverse(device, bit_count) + jnp.arange(2, dtype=jnp.int32)
    total_points = 2 * parts_count * tokens
    column_index = jnp.arange(tokens, dtype=jnp.int32)
    full_freq = coarse_freq[:, None] + 2 * parts_count * column_index[None, :]
    phase_value = column_index[None, None, :] * full_freq[:, :, None] % total_points
    angle_value = phase_value.astype(jnp.float32) * (2.0 * math.pi / total_points)
    return (jnp.cos(angle_value), -jnp.sin(angle_value))


def contract(matrix, values):
    return jnp.einsum("akm,amw->akw", matrix, values, precision=PRECISE)


def contract_back(matrix, values):
    return jnp.einsum("akm,akw->amw", matrix, values, precision=PRECISE)


def local_forward(spec_real, spec_imag, table):
    table_real, table_imag = table
    out_real = contract(table_real, spec_real) - contract(table_imag, spec_imag)
    out_imag = contract(table_real, spec_imag) + contract(table_imag, spec_real)
    return (out_real, out_imag)


def local_inverse(spec_real, spec_imag, table):
    table_real, table_imag = table
    factor = 1.0 / spec_real.shape[1]
    out_real = (
        contract_back(table_real, spec_real) + contract_back(table_imag, spec_imag)
    ) * factor
    out_imag = (
        contract_back(table_real, spec_imag) - contract_back(table_imag, spec_real)
    ) * factor
    return (out_real, out_imag)


def pair_swap(stacked, bit_place):
    return swapped(stacked, "ctx", bit_place)


def pair_swap_back(stacked, bit_place):
    return swapped(stacked, "ctx", bit_place)


def section_terms(device, bit_place):
    span_size = 2**bit_place
    upper_flag = device // span_size % 2
    sign_value = (1 - 2 * upper_flag).astype(jnp.float32)
    turn_value = math.pi / span_size * (upper_flag * (device % span_size)).astype(jnp.float32)
    return (sign_value, jnp.cos(turn_value), jnp.sin(turn_value))


def butterfly_forward(signals):
    parts_count = lax.axis_size("ctx")
    device = lax.axis_index("ctx")
    bit_count = parts_count.bit_length() - 1
    angle_value = math.pi * device.astype(jnp.float32) / parts_count
    spec_real = jnp.stack([signals, signals * jnp.cos(angle_value)])
    spec_imag = jnp.stack([jnp.zeros_like(signals), -signals * jnp.sin(angle_value)])
    for bit_place in reversed(range(bit_count)):
        sign_value, cos_turn, sin_turn = section_terms(device, bit_place)
        partner = pair_swap(jnp.stack([spec_real, spec_imag]), bit_place)
        joined_real = partner[0] + sign_value * spec_real
        joined_imag = partner[1] + sign_value * spec_imag
        spec_real = joined_real * cos_turn + joined_imag * sin_turn
        spec_imag = joined_imag * cos_turn - joined_real * sin_turn
    return (spec_real, spec_imag)


def butterfly_inverse(spec_real, spec_imag):
    parts_count = lax.axis_size("ctx")
    device = lax.axis_index("ctx")
    bit_count = parts_count.bit_length() - 1
    for bit_place in range(bit_count):
        sign_value, cos_turn, sin_turn = section_terms(device, bit_place)
        turned_real = spec_real * cos_turn - spec_imag * sin_turn
        turned_imag = spec_imag * cos_turn + spec_real * sin_turn
        partner = pair_swap_back(jnp.stack([turned_real, turned_imag]), bit_place)
        spec_real = 0.5 * (partner[0] + sign_value * turned_real)
        spec_imag = 0.5 * (partner[1] + sign_value * turned_imag)
    angle_value = math.pi * device.astype(jnp.float32) / parts_count
    cos_last = jnp.cos(angle_value)
    sin_last = jnp.sin(angle_value)
    out_real = 0.5 * (spec_real[0] + spec_real[1] * cos_last - spec_imag[1] * sin_last)
    out_imag = 0.5 * (spec_imag[0] + spec_imag[1] * cos_last + spec_real[1] * sin_last)
    return (out_real, out_imag)


def per_device(features, short_weight, long_filter, skip_bias, cotangent):
    taps = short_weight.shape[0]
    token_rows = features[0]
    tokens = token_rows.shape[0]
    channels = long_filter.shape[1]
    parts_count = lax.axis_size("ctx")
    device = lax.axis_index("ctx")
    history = shifted(token_rows[tokens - (taps - 1) :], "ctx", 1)
    extended = jnp.concatenate([history, token_rows], axis=0).astype(jnp.float32)
    mixed_feats = jnp.zeros((tokens, token_rows.shape[1]), jnp.float32)
    for tap_index in range(taps):
        start_row = taps - 1 - tap_index
        mixed_feats = (
            mixed_feats + short_weight[tap_index] * extended[start_row : start_row + tokens]
        )
    query = mixed_feats[:, :channels]
    key_part = mixed_feats[:, channels : 2 * channels]
    value_part = mixed_feats[:, 2 * channels :]
    gated = key_part * value_part
    upstream = cotangent[0].astype(jnp.float32)
    dconv = upstream * query
    signals = jnp.concatenate([gated, long_filter, dconv], axis=1)
    table = spectral_table(device, parts_count, tokens)
    spec_real, spec_imag = butterfly_forward(signals)
    spec_real, spec_imag = local_forward(spec_real, spec_imag, table)
    gated_real = spec_real[..., :channels]
    gated_imag = spec_imag[..., :channels]
    filter_real = spec_real[..., channels : 2 * channels]
    filter_imag = spec_imag[..., channels : 2 * channels]
    dconv_real = spec_real[..., 2 * channels :]
    dconv_imag = spec_imag[..., 2 * channels :]
    conv_real = gated_real * filter_real - gated_imag * filter_imag
    conv_imag = gated_real * filter_imag + gated_imag * filter_real
    back_real = filter_real * dconv_real + filter_imag * dconv_imag
    back_imag = filter_real * dconv_imag - filter_imag * dconv_real
    corr_real = gated_real * dconv_real + gated_imag * dconv_imag
    corr_imag = gated_real * dconv_imag - gated_imag * dconv_real
    inverse_real = jnp.concatenate([conv_real - back_imag, corr_real], axis=-1)
    inverse_imag = jnp.concatenate([conv_imag + back_real, corr_imag], axis=-1)
    inverse_real, inverse_imag = local_inverse(inverse_real, inverse_imag, table)
    result_real, result_imag = butterfly_inverse(inverse_real, inverse_imag)
    long_conv = result_real[:, :channels] + skip_bias * gated
    dgated = result_imag[:, :channels] + skip_bias * dconv
    filter_part = result_real[:, channels:]
    layer_out = (query * long_conv).astype(jnp.bfloat16)[None]
    dmixed = jnp.concatenate([upstream * long_conv, dgated * value_part, dgated * key_part], axis=1)
    later = shifted(dmixed[: taps - 1], "ctx", -1)
    ahead = jnp.concatenate([dmixed, later], axis=0)
    grad_local = jnp.zeros_like(dmixed)
    short_rows = []
    for tap_index in range(taps):
        grad_local = grad_local + short_weight[tap_index] * ahead[tap_index : tap_index + tokens]
        start_row = taps - 1 - tap_index
        short_rows.append(jnp.sum(dmixed * extended[start_row : start_row + tokens], axis=0))
    grad_features = grad_local.astype(jnp.bfloat16)[None]
    short_part = jnp.stack(short_rows)
    skip_part = jnp.sum(dconv * gated, axis=0)
    scale = 1.0 / math.sqrt(lax.axis_size("dp") * parts_count * tokens)
    filter_sum = lax.psum(filter_part, "dp")
    short_sum, skip_sum = lax.psum((short_part, skip_part), ("dp", "ctx"))
    return (layer_out, grad_features, short_sum * scale, filter_sum * scale, skip_sum * scale)


def solution(mesh):
    return jax.shard_map(
        per_device,
        mesh=mesh,
        in_specs=(P("dp", "ctx", None), P(), P("ctx", None), P(), P("dp", "ctx", None)),
        out_specs=(P("dp", "ctx", None), P("dp", "ctx", None), P(), P("ctx", None), P()),
        check_vma=False,
    )
```

profile of v0, /device:TPU:2, one launch (start us, length us, event | category | flops | bytes accessed | tf_op | source)
XLA Modules:
  0.0 1050.0 jit_solution(7923902592177502704)
XLA Ops:
  8.0 3.8 collective-permute-start
  13.2 4.3 collective-permute-done
  23.9 2.4 collective-permute-start.1
  26.5 68.2 %collective-permute-done.1 = f32[2,2,128,1536]{3,2,1,0:T(8,128)} collective-permute-done((f32[2,2,128,1536]{3,2,1,0:T(8,128)}, f32[2,2,128,1536]{3,2,1,0:T(8,128)}, u32[]{:S(2)}, u32[]{:S(2)}) %collective-permute-start.1) | collective-permute-done | bytes 3145760 | tf_op jit(solution)/shard_map/ppermute | solution.py:13
  94.7 3.0 multiply_subtract_fusion.4
  97.7 2.0 pad_maximum_fusion.1
  100.3 67.9 %collective-permute-done.2 = f32[2,2,128,1536]{3,2,1,0:T(8,128)} collective-permute-done((f32[2,2,128,1536]{3,2,1,0:T(8,128)}, f32[2,2,128,1536]{3,2,1,0:T(8,128)}, u32[]{:S(2)}, u32[]{:S(2)}) %collective-permute-start.2) | collective-permute-done | bytes 3145760 | tf_op jit(solution)/shard_map/ppermute | solution.py:13
  168.2 3.1 multiply_subtract_fusion.3
  171.3 2.1 pad_maximum_fusion.2
  174.0 4.0 collective-permute-start.3
  178.1 135.4 %collective-permute-done.3 = f32[2,2,128,1536]{3,2,1,0:T(8,128)} collective-permute-done((f32[2,2,128,1536]{3,2,1,0:T(8,128)}, f32[2,2,128,1536]{3,2,1,0:T(8,128)}, u32[]{:S(2)}, u32[]{:S(2)}) %collective-permute-start.3) | collective-permute-done | bytes 3145760 | tf_op jit(solution)/shard_map/ppermute | solution.py:13
  313.5 3.6 multiply_subtract_fusion.2
  317.1 2.1 pad_maximum_fusion.3
  319.4 137.3 %collective-permute-done.4 = f32[2,2,128,1536]{3,2,1,0:T(8,128)} collective-permute-done((f32[2,2,128,1536]{3,2,1,0:T(8,128)}, f32[2,2,128,1536]{3,2,1,0:T(8,128)}, u32[]{:S(2)}, u32[]{:S(2)}) %collective-permute-start.4) | collective-permute-done | bytes 3145760 | tf_op jit(solution)/shard_map/ppermute | solution.py:13
  456.7 3.1 multiply_add_fusion.1
  462.6 69.4 %collective-permute-done.5 = f32[2,2,128,1536]{3,2,1,0:T(8,128)} collective-permute-done((f32[2,2,128,1536]{3,2,1,0:T(8,128)}, f32[2,2,128,1536]{3,2,1,0:T(8,128)}, u32[]{:S(2)}, u32[]{:S(2)}) %collective-permute-start.5) | collective-permute-done | bytes 3145760 | tf_op jit(solution)/shard_map/ppermute | solution.py:13
  532.0 3.5 fusion.2
  552.4 45.8 %collective-permute-done.6 = f32[2,2,128,1024]{3,2,1,0:T(8,128)} collective-permute-done((f32[2,2,128,1024]{3,2,1,0:T(8,128)}, f32[2,2,128,1024]{3,2,1,0:T(8,128)}, u32[]{:S(2)}, u32[]{:S(2)}) %collective-permute-start.6) | collective-permute-done | bytes 2097184 | tf_op jit(solution)/shard_map/ppermute | solution.py:13
  598.2 2.0 multiply_add_fusion.8
  602.7 2.1 collective-permute-start.7
  604.8 89.6 %collective-permute-done.7 = f32[2,2,128,1024]{3,2,1,0:T(8,128)} collective-permute-done((f32[2,2,128,1024]{3,2,1,0:T(8,128)}, f32[2,2,128,1024]{3,2,1,0:T(8,128)}, u32[]{:S(2)}, u32[]{:S(2)}) %collective-permute-start.7) | collective-permute-done | bytes 2097184 | tf_op jit(solution)/shard_map/ppermute | solution.py:13
  694.5 2.3 multiply_add_fusion.7
  698.1 3.7 collective-permute-start.8
  701.8 92.3 %collective-permute-done.8 = f32[2,2,128,1024]{3,2,1,0:T(8,128)} collective-permute-done((f32[2,2,128,1024]{3,2,1,0:T(8,128)S(1)}, f32[2,2,128,1024]{3,2,1,0:T(8,128)}, u32[]{:S(2)}, u32[]{:S(2)}) %collective-permute-start.8) | collective-permute-done | bytes 2097184 | tf_op jit(solution)/shard_map/ppermute | solution.py:13
  794.1 2.7 multiply_add_fusion.6
  799.2 46.3 %collective-permute-done.9 = f32[2,2,128,1024]{3,2,1,0:T(8,128)} collective-permute-done((f32[2,2,128,1024]{3,2,1,0:T(8,128)}, f32[2,2,128,1024]{3,2,1,0:T(8,128)}, u32[]{:S(2)}, u32[]{:S(2)}) %collective-permute-start.9) | collective-permute-done | bytes 2097184 | tf_op jit(solution)/shard_map/ppermute | solution.py:13
  845.5 2.0 multiply_subtract_fusion.5
  847.8 3.2 collective-permute-start.10
  851.0 45.0 %collective-permute-done.10 = f32[2,2,128,1024]{3,2,1,0:T(8,128)S(1)} collective-permute-done((f32[2,2,128,1024]{3,2,1,0:T(8,128)S(1)}, f32[2,2,128,1024]{3,2,1,0:T(8,128)S(1)}, u32[]{:S(2)}, u32[]{:S(2)}) %collective-permute-start.10) | collective-permute-done | bytes 2097184 | tf_op jit(solution)/shard_map/ppermute | solution.py:13
  899.7 75.3 %all-reduce.1 = (f32[7,1536]{1,0:T(8,128)S(1)}, f32[512]{0:T(512)S(1)}) all-reduce(f32[7,1536]{1,0:T(8,128)S(1)} %stack.165, f32[512]{0:T(512)S(1)} %get-tuple-element.21), channel_id=1, replica_groups=mesh['dp'=8,'ctx'=32] {'dp','ctx'}, use_global_device_ids=true, to_apply=%region_7.8 | all-reduce | flops 11264 | bytes 90112 | tf_op jit(solution)/shard_map/psum | solution.py:179
  975.7 4.7 collective-permute-start.11
  983.7 57.8 %all-reduce.4.cloned.1.call-done = f32[128,512]{1,0:T(8,128)} async-done(((f32[128,512]{1,0:T(8,128)}), f32[128,512]{1,0:T(8,128)}) %all-reduce.4.cloned.1.call-update) | async-done | bytes 262160 | tf_op jit(solution)/shard_map/psum | solution.py:178
  (94 shorter events, 44.5 us)
Async XLA Ops:
  7.2 1034.3 %all-reduce.4.cloned.1.call-start = ((), (), s32[]{:S(2)}) async-start(), calls=%async_computation | async-start | bytes 524288 | tf_op jit(solution)/shard_map/psum | solution.py:178
  8.0 9.5 collective-permute-start
  18.6 0.9 copy-start.16
  19.5 1.4 copy-start.9
  19.5 1.1 copy-start.15
  19.6 1.3 copy-start.13
  20.9 0.9 copy-start.11
  20.9 1.1 copy-start.12
  23.9 70.8 %collective-permute-start.1 = (f32[2,2,128,1536]{3,2,1,0:T(8,128)}, f32[2,2,128,1536]{3,2,1,0:T(8,128)}, u32[]{:S(2)}, u32[]{:S(2)}) collective-permute-start(f32[2,2,128,1536]{3,2,1,0:T(8,128)} %pad_maximum_fusion), channel_id=1, source_target_pairs={{0,16},{1,17},{2,18},{3,19},{4,20},{5,21},{6,22},{7,23},{8,24},{9,... | collective-permute-start | bytes 9437192 | tf_op jit(solution)/shard_map/ppermute | solution.py:13
  97.7 2.1 copy-start.1
  99.8 68.4 %collective-permute-start.2 = (f32[2,2,128,1536]{3,2,1,0:T(8,128)}, f32[2,2,128,1536]{3,2,1,0:T(8,128)}, u32[]{:S(2)}, u32[]{:S(2)}) collective-permute-start(f32[2,2,128,1536]{3,2,1,0:T(8,128)} %pad_maximum_fusion.1), channel_id=1, source_target_pairs={{0,8},{1,9},{2,10},{3,11},{4,12},{5,13},{6,14},{7,15},{8,0},{9,1},... | collective-permute-start | bytes 9437192 | tf_op jit(solution)/shard_map/ppermute | solution.py:13
  171.3 2.3 copy-start.2
  171.3 2.7 copy-start.3
  174.0 139.6 %collective-permute-start.3 = (f32[2,2,128,1536]{3,2,1,0:T(8,128)}, f32[2,2,128,1536]{3,2,1,0:T(8,128)}, u32[]{:S(2)}, u32[]{:S(2)}) collective-permute-start(f32[2,2,128,1536]{3,2,1,0:T(8,128)} %pad_maximum_fusion.2), channel_id=1, source_target_pairs={{0,4},{1,5},{2,6},{3,7},{4,0},{5,1},{6,2},{7,3},{8,12},{9,13},{10,... | collective-permute-start | bytes 9437192 | tf_op jit(solution)/shard_map/ppermute | solution.py:13
  317.1 2.1 copy-start
  319.3 137.4 %collective-permute-start.4 = (f32[2,2,128,1536]{3,2,1,0:T(8,128)}, f32[2,2,128,1536]{3,2,1,0:T(8,128)}, u32[]{:S(2)}, u32[]{:S(2)}) collective-permute-start(f32[2,2,128,1536]{3,2,1,0:T(8,128)} %pad_maximum_fusion.3), channel_id=1, source_target_pairs={{0,2},{1,3},{2,0},{3,1},{4,6},{5,7},{6,4},{7,5},{8,10},{9,11},{10,... | collective-permute-start | bytes 9437192 | tf_op jit(solution)/shard_map/ppermute | solution.py:13
  459.8 2.1 copy-start.4
  459.8 2.7 copy-start.5
  462.5 69.5 %collective-permute-start.5 = (f32[2,2,128,1536]{3,2,1,0:T(8,128)}, f32[2,2,128,1536]{3,2,1,0:T(8,128)}, u32[]{:S(2)}, u32[]{:S(2)}) collective-permute-start(f32[2,2,128,1536]{3,2,1,0:T(8,128)} %pad_maximum_fusion.4), channel_id=1, source_target_pairs={{0,1},{1,0},{2,3},{3,2},{4,5},{5,4},{6,7},{7,6},{8,9},{9,8},{10,11... | collective-permute-start | bytes 9437192 | tf_op jit(solution)/shard_map/ppermute | solution.py:13
  552.1 46.1 %collective-permute-start.6 = (f32[2,2,128,1024]{3,2,1,0:T(8,128)}, f32[2,2,128,1024]{3,2,1,0:T(8,128)}, u32[]{:S(2)}, u32[]{:S(2)}) collective-permute-start(f32[2,2,128,1024]{3,2,1,0:T(8,128)} %pad_maximum_fusion.5), channel_id=1, source_target_pairs={{0,1},{1,0},{2,3},{3,2},{4,5},{5,4},{6,7},{7,6},{8,9},{9,8},{10,11... | collective-permute-start | bytes 6291464 | tf_op jit(solution)/shard_map/ppermute | solution.py:13
  600.3 1.0 copy-start.6
  602.7 91.7 %collective-permute-start.7 = (f32[2,2,128,1024]{3,2,1,0:T(8,128)}, f32[2,2,128,1024]{3,2,1,0:T(8,128)}, u32[]{:S(2)}, u32[]{:S(2)}) collective-permute-start(f32[2,2,128,1024]{3,2,1,0:T(8,128)} %pad_maximum_fusion.6), channel_id=1, source_target_pairs={{0,2},{1,3},{2,0},{3,1},{4,6},{5,7},{6,4},{7,5},{8,10},{9,11},{10,... | collective-permute-start | bytes 6291464 | tf_op jit(solution)/shard_map/ppermute | solution.py:13
  696.8 1.0 copy-start.7
  696.8 1.3 copy-start.8
  698.1 96.0 %collective-permute-start.8 = (f32[2,2,128,1024]{3,2,1,0:T(8,128)S(1)}, f32[2,2,128,1024]{3,2,1,0:T(8,128)}, u32[]{:S(2)}, u32[]{:S(2)}) collective-permute-start(f32[2,2,128,1024]{3,2,1,0:T(8,128)S(1)} %pad_maximum_fusion.7), channel_id=1, source_target_pairs={{0,4},{1,5},{2,6},{3,7},{4,0},{5,1},{6,2},{7,3},{8,12},{9,13},{10,... | collective-permute-start | bytes 6291464 | tf_op jit(solution)/shard_map/ppermute | solution.py:13
  798.3 47.3 %collective-permute-start.9 = (f32[2,2,128,1024]{3,2,1,0:T(8,128)}, f32[2,2,128,1024]{3,2,1,0:T(8,128)}, u32[]{:S(2)}, u32[]{:S(2)}) collective-permute-start(f32[2,2,128,1024]{3,2,1,0:T(8,128)} %pad_maximum_fusion.8), channel_id=1, source_target_pairs={{0,8},{1,9},{2,10},{3,11},{4,12},{5,13},{6,14},{7,15},{8,0},{9,1},... | collective-permute-start | bytes 6291464 | tf_op jit(solution)/shard_map/ppermute | solution.py:13
  847.8 48.2 %collective-permute-start.10 = (f32[2,2,128,1024]{3,2,1,0:T(8,128)S(1)}, f32[2,2,128,1024]{3,2,1,0:T(8,128)S(1)}, u32[]{:S(2)}, u32[]{:S(2)}) collective-permute-start(f32[2,2,128,1024]{3,2,1,0:T(8,128)S(1)} %pad_maximum_fusion.9), channel_id=1, source_target_pairs={{0,16},{1,17},{2,18},{3,19},{4,20},{5,21},{6,22},{7,23},{8,24},{9,... | collective-permute-start | bytes 6291464 | tf_op jit(solution)/shard_map/ppermute | solution.py:13
  896.6 1.1 copy-start.10
  896.6 1.2 copy-start.14
  896.6 1.2 copy-start.17
  896.7 1.2 copy-start.18
  975.7 6.5 collective-permute-start.11
Sparse Core Ops, SparseCore 0:
  981.2 60.1 all-reduce.3
where the time goes:
time: 1050 us
  waiting for transfers between devices  860 us (82%)
  blocking collectives  75.3 us (7%)
  other arithmetic  50.7 us (5%)
  starting transfers between devices  25.6 us (2%)
  between operations  15.3 us (1%)
  matrix products  14.2 us (1%)
    ppermute x10, waiting for transfers between devices, swapped(): return lax.ppermute(value, axis, pairs)  797 us
    psum x1, blocking collectives, per_device(): short_sum, skip_sum = lax.psum((short_part, skip_part), ('dp', 'ctx'))  75.3 us
    psum x1, waiting for transfers between devices, per_device(): filter_sum = lax.psum(filter_part, 'dp')  57.8 us
  transfers between devices with their start and end apart: 13, of which 13 were waited for; matrix products, arithmetic and copies ran while one was open for 0% of the time, Pallas kernels for 0%

commit v1 on v0

--- a/solution.py
+++ b/solution.py
@@ -3,6 +3,7 @@
 import jax.numpy as jnp
 from jax import lax
 from jax.sharding import PartitionSpec as P
+from jax.lax import all_gather
 
 PRECISE = lax.Precision.HIGHEST
 
@@ -175,7 +176,8 @@
     short_part = jnp.stack(short_rows)
     skip_part = jnp.sum(dconv * gated, axis=0)
     scale = 1.0 / math.sqrt(lax.axis_size("dp") * parts_count * tokens)
-    filter_sum = lax.psum(filter_part, "dp")
+    plain = all_gather(filter_part, "dp")
+    filter_sum = jnp.sum(plain, axis=0)
     short_sum, skip_sum = lax.psum((short_part, skip_part), ("dp", "ctx"))
     return (layer_out, grad_features, short_sum * scale, filter_sum * scale, skip_sum * scale)
 

time: 1050 us -> 992 us (0.945)
  waiting for transfers between devices: 860 us -> 802 us
    psum x1 -> x0, waiting for transfers between devices: 57.8 us -> none  [per_device(): filter_sum = lax.psum(filter_part, 'dp')]
  transfers between devices with their start and end apart: 13 -> 13, of which waited for: 13 -> 11; matrix products, arithmetic and copies ran while one was open for 0% -> 0% of each run, Pallas kernels for 0% -> 0%
where the time goes in v1:
time: 992 us; the launch traced here: 990 us
  waiting for transfers between devices  802 us (81%)
  blocking collectives  75 us (8%)
  other arithmetic  51.6 us (5%)
  starting transfers between devices  24.2 us (2%)
  between operations  15.3 us (2%)
  matrix products  14.2 us (1%)
    ppermute x10, waiting for transfers between devices, swapped(): return lax.ppermute(value, axis, pairs)  797 us
    psum x1, blocking collectives, per_device(): short_sum, skip_sum = lax.psum((short_part, skip_part), ('dp', 'ctx'))  75 us
  transfers between devices with their start and end apart: 13, of which 11 were waited for; matrix products, arithmetic and copies ran while one was open for 0% of the time, Pallas kernels for 0%

profile of v1, /device:TPU:2, one launch (start us, length us, event | category | flops | bytes accessed | tf_op | source)
XLA Modules:
  0.0 990.3 jit_solution(6829172601875964276)
XLA Ops:
  8.0 3.8 collective-permute-start
  13.2 4.3 collective-permute-done
  23.9 2.4 collective-permute-start.1
  26.5 68.2 %collective-permute-done.1 = f32[2,2,128,1536]{3,2,1,0:T(8,128)} collective-permute-done((f32[2,2,128,1536]{3,2,1,0:T(8,128)}, f32[2,2,128,1536]{3,2,1,0:T(8,128)}, u32[]{:S(2)}, u32[]{:S(2)}) %collective-permute-start.1) | collective-permute-done | bytes 3145760 | tf_op jit(solution)/shard_map/ppermute | solution.py:14
  94.7 3.0 multiply_subtract_fusion.4
  97.7 2.0 pad_maximum_fusion.1
  100.3 67.9 %collective-permute-done.2 = f32[2,2,128,1536]{3,2,1,0:T(8,128)} collective-permute-done((f32[2,2,128,1536]{3,2,1,0:T(8,128)}, f32[2,2,128,1536]{3,2,1,0:T(8,128)}, u32[]{:S(2)}, u32[]{:S(2)}) %collective-permute-start.2) | collective-permute-done | bytes 3145760 | tf_op jit(solution)/shard_map/ppermute | solution.py:14
  168.2 3.1 multiply_subtract_fusion.3
  171.3 2.1 pad_maximum_fusion.2
  174.0 4.0 collective-permute-start.3
  178.1 135.4 %collective-permute-done.3 = f32[2,2,128,1536]{3,2,1,0:T(8,128)} collective-permute-done((f32[2,2,128,1536]{3,2,1,0:T(8,128)}, f32[2,2,128,1536]{3,2,1,0:T(8,128)}, u32[]{:S(2)}, u32[]{:S(2)}) %collective-permute-start.3) | collective-permute-done | bytes 3145760 | tf_op jit(solution)/shard_map/ppermute | solution.py:14
  313.5 3.6 multiply_subtract_fusion.2
  317.1 2.1 pad_maximum_fusion.3
  319.4 137.3 %collective-permute-done.4 = f32[2,2,128,1536]{3,2,1,0:T(8,128)} collective-permute-done((f32[2,2,128,1536]{3,2,1,0:T(8,128)}, f32[2,2,128,1536]{3,2,1,0:T(8,128)}, u32[]{:S(2)}, u32[]{:S(2)}) %collective-permute-start.4) | collective-permute-done | bytes 3145760 | tf_op jit(solution)/shard_map/ppermute | solution.py:14
  456.7 3.1 multiply_add_fusion.1
  459.8 2.0 pad_maximum_fusion.4
  462.6 69.4 %collective-permute-done.5 = f32[2,2,128,1536]{3,2,1,0:T(8,128)} collective-permute-done((f32[2,2,128,1536]{3,2,1,0:T(8,128)}, f32[2,2,128,1536]{3,2,1,0:T(8,128)}, u32[]{:S(2)}, u32[]{:S(2)}) %collective-permute-start.5) | collective-permute-done | bytes 3145760 | tf_op jit(solution)/shard_map/ppermute | solution.py:14
  532.0 3.5 fusion.2
  552.4 45.8 %collective-permute-done.6 = f32[2,2,128,1024]{3,2,1,0:T(8,128)} collective-permute-done((f32[2,2,128,1024]{3,2,1,0:T(8,128)}, f32[2,2,128,1024]{3,2,1,0:T(8,128)}, u32[]{:S(2)}, u32[]{:S(2)}) %collective-permute-start.6) | collective-permute-done | bytes 2097184 | tf_op jit(solution)/shard_map/ppermute | solution.py:14
  598.2 2.0 multiply_add_fusion.8
  602.7 2.1 collective-permute-start.7
  604.8 89.6 %collective-permute-done.7 = f32[2,2,128,1024]{3,2,1,0:T(8,128)} collective-permute-done((f32[2,2,128,1024]{3,2,1,0:T(8,128)}, f32[2,2,128,1024]{3,2,1,0:T(8,128)}, u32[]{:S(2)}, u32[]{:S(2)}) %collective-permute-start.7) | collective-permute-done | bytes 2097184 | tf_op jit(solution)/shard_map/ppermute | solution.py:14
  694.5 2.3 multiply_add_fusion.7
  698.1 3.7 collective-permute-start.8
  701.8 92.3 %collective-permute-done.8 = f32[2,2,128,1024]{3,2,1,0:T(8,128)} collective-permute-done((f32[2,2,128,1024]{3,2,1,0:T(8,128)S(1)}, f32[2,2,128,1024]{3,2,1,0:T(8,128)}, u32[]{:S(2)}, u32[]{:S(2)}) %collective-permute-start.8) | collective-permute-done | bytes 2097184 | tf_op jit(solution)/shard_map/ppermute | solution.py:14
  794.1 2.7 multiply_add_fusion.6
  799.2 46.3 %collective-permute-done.9 = f32[2,2,128,1024]{3,2,1,0:T(8,128)} collective-permute-done((f32[2,2,128,1024]{3,2,1,0:T(8,128)}, f32[2,2,128,1024]{3,2,1,0:T(8,128)}, u32[]{:S(2)}, u32[]{:S(2)}) %collective-permute-start.9) | collective-permute-done | bytes 2097184 | tf_op jit(solution)/shard_map/ppermute | solution.py:14
  845.5 2.0 multiply_subtract_fusion.5
  847.8 3.2 collective-permute-start.10
  851.0 45.0 %collective-permute-done.10 = f32[2,2,128,1024]{3,2,1,0:T(8,128)S(1)} collective-permute-done((f32[2,2,128,1024]{3,2,1,0:T(8,128)S(1)}, f32[2,2,128,1024]{3,2,1,0:T(8,128)S(1)}, u32[]{:S(2)}, u32[]{:S(2)}) %collective-permute-start.10) | collective-permute-done | bytes 2097184 | tf_op jit(solution)/shard_map/ppermute | solution.py:14
  899.7 3.4 collective-permute-start.11
  903.2 75.0 %all-reduce.1 = (f32[7,1536]{1,0:T(8,128)S(1)}, f32[512]{0:T(512)S(1)}) all-reduce(f32[7,1536]{1,0:T(8,128)S(1)} %stack.165, f32[512]{0:T(512)S(1)} %get-tuple-element.21), channel_id=1, replica_groups=mesh['dp'=8,'ctx'=32] {'dp','ctx'}, use_global_device_ids=true, to_apply=%region_7.8 | all-reduce | flops 11264 | bytes 90112 | tf_op jit(solution)/shard_map/psum | solution.py:181
  (95 shorter events, 42.3 us)
Async XLA Ops:
  7.2 973.7 %all-gather.3.cloned.1.call-start = ((), (), s32[]{:S(2)}) async-start(), calls=%async_computation | async-start | bytes 2359296 | tf_op jit(solution)/shard_map/all_gather | solution.py:179
  8.0 9.5 collective-permute-start
  18.6 0.9 copy-start.16
  19.5 1.4 copy-start.9
  19.5 1.1 copy-start.15
  19.6 1.3 copy-start.13
  20.9 0.9 copy-start.11
  20.9 1.1 copy-start.12
  23.9 70.8 %collective-permute-start.1 = (f32[2,2,128,1536]{3,2,1,0:T(8,128)}, f32[2,2,128,1536]{3,2,1,0:T(8,128)}, u32[]{:S(2)}, u32[]{:S(2)}) collective-permute-start(f32[2,2,128,1536]{3,2,1,0:T(8,128)} %pad_maximum_fusion), channel_id=1, source_target_pairs={{0,16},{1,17},{2,18},{3,19},{4,20},{5,21},{6,22},{7,23},{8,24},{9,... | collective-permute-start | bytes 9437192 | tf_op jit(solution)/shard_map/ppermute | solution.py:14
  97.7 2.1 copy-start.1
  99.8 68.4 %collective-permute-start.2 = (f32[2,2,128,1536]{3,2,1,0:T(8,128)}, f32[2,2,128,1536]{3,2,1,0:T(8,128)}, u32[]{:S(2)}, u32[]{:S(2)}) collective-permute-start(f32[2,2,128,1536]{3,2,1,0:T(8,128)} %pad_maximum_fusion.1), channel_id=1, source_target_pairs={{0,8},{1,9},{2,10},{3,11},{4,12},{5,13},{6,14},{7,15},{8,0},{9,1},... | collective-permute-start | bytes 9437192 | tf_op jit(solution)/shard_map/ppermute | solution.py:14
  171.3 2.3 copy-start.2
  171.3 2.7 copy-start.3
  174.0 139.6 %collective-permute-start.3 = (f32[2,2,128,1536]{3,2,1,0:T(8,128)}, f32[2,2,128,1536]{3,2,1,0:T(8,128)}, u32[]{:S(2)}, u32[]{:S(2)}) collective-permute-start(f32[2,2,128,1536]{3,2,1,0:T(8,128)} %pad_maximum_fusion.2), channel_id=1, source_target_pairs={{0,4},{1,5},{2,6},{3,7},{4,0},{5,1},{6,2},{7,3},{8,12},{9,13},{10,... | collective-permute-start | bytes 9437192 | tf_op jit(solution)/shard_map/ppermute | solution.py:14
  317.1 2.1 copy-start
  319.3 137.4 %collective-permute-start.4 = (f32[2,2,128,1536]{3,2,1,0:T(8,128)}, f32[2,2,128,1536]{3,2,1,0:T(8,128)}, u32[]{:S(2)}, u32[]{:S(2)}) collective-permute-start(f32[2,2,128,1536]{3,2,1,0:T(8,128)} %pad_maximum_fusion.3), channel_id=1, source_target_pairs={{0,2},{1,3},{2,0},{3,1},{4,6},{5,7},{6,4},{7,5},{8,10},{9,11},{10,... | collective-permute-start | bytes 9437192 | tf_op jit(solution)/shard_map/ppermute | solution.py:14
  459.8 2.1 copy-start.4
  459.8 2.7 copy-start.5
  462.5 69.5 %collective-permute-start.5 = (f32[2,2,128,1536]{3,2,1,0:T(8,128)}, f32[2,2,128,1536]{3,2,1,0:T(8,128)}, u32[]{:S(2)}, u32[]{:S(2)}) collective-permute-start(f32[2,2,128,1536]{3,2,1,0:T(8,128)} %pad_maximum_fusion.4), channel_id=1, source_target_pairs={{0,1},{1,0},{2,3},{3,2},{4,5},{5,4},{6,7},{7,6},{8,9},{9,8},{10,11... | collective-permute-start | bytes 9437192 | tf_op jit(solution)/shard_map/ppermute | solution.py:14
  552.1 46.1 %collective-permute-start.6 = (f32[2,2,128,1024]{3,2,1,0:T(8,128)}, f32[2,2,128,1024]{3,2,1,0:T(8,128)}, u32[]{:S(2)}, u32[]{:S(2)}) collective-permute-start(f32[2,2,128,1024]{3,2,1,0:T(8,128)} %pad_maximum_fusion.5), channel_id=1, source_target_pairs={{0,1},{1,0},{2,3},{3,2},{4,5},{5,4},{6,7},{7,6},{8,9},{9,8},{10,11... | collective-permute-start | bytes 6291464 | tf_op jit(solution)/shard_map/ppermute | solution.py:14
  600.3 1.0 copy-start.6
  602.7 91.7 %collective-permute-start.7 = (f32[2,2,128,1024]{3,2,1,0:T(8,128)}, f32[2,2,128,1024]{3,2,1,0:T(8,128)}, u32[]{:S(2)}, u32[]{:S(2)}) collective-permute-start(f32[2,2,128,1024]{3,2,1,0:T(8,128)} %pad_maximum_fusion.6), channel_id=1, source_target_pairs={{0,2},{1,3},{2,0},{3,1},{4,6},{5,7},{6,4},{7,5},{8,10},{9,11},{10,... | collective-permute-start | bytes 6291464 | tf_op jit(solution)/shard_map/ppermute | solution.py:14
  696.8 1.0 copy-start.7
  696.8 1.3 copy-start.8
  698.1 96.0 %collective-permute-start.8 = (f32[2,2,128,1024]{3,2,1,0:T(8,128)S(1)}, f32[2,2,128,1024]{3,2,1,0:T(8,128)}, u32[]{:S(2)}, u32[]{:S(2)}) collective-permute-start(f32[2,2,128,1024]{3,2,1,0:T(8,128)S(1)} %pad_maximum_fusion.7), channel_id=1, source_target_pairs={{0,4},{1,5},{2,6},{3,7},{4,0},{5,1},{6,2},{7,3},{8,12},{9,13},{10,... | collective-permute-start | bytes 6291464 | tf_op jit(solution)/shard_map/ppermute | solution.py:14
  798.3 47.3 %collective-permute-start.9 = (f32[2,2,128,1024]{3,2,1,0:T(8,128)}, f32[2,2,128,1024]{3,2,1,0:T(8,128)}, u32[]{:S(2)}, u32[]{:S(2)}) collective-permute-start(f32[2,2,128,1024]{3,2,1,0:T(8,128)} %pad_maximum_fusion.8), channel_id=1, source_target_pairs={{0,8},{1,9},{2,10},{3,11},{4,12},{5,13},{6,14},{7,15},{8,0},{9,1},... | collective-permute-start | bytes 6291464 | tf_op jit(solution)/shard_map/ppermute | solution.py:14
  847.8 48.2 %collective-permute-start.10 = (f32[2,2,128,1024]{3,2,1,0:T(8,128)S(1)}, f32[2,2,128,1024]{3,2,1,0:T(8,128)S(1)}, u32[]{:S(2)}, u32[]{:S(2)}) collective-permute-start(f32[2,2,128,1024]{3,2,1,0:T(8,128)S(1)} %pad_maximum_fusion.9), channel_id=1, source_target_pairs={{0,16},{1,17},{2,18},{3,19},{4,20},{5,21},{6,22},{7,23},{8,24},{9,... | collective-permute-start | bytes 6291464 | tf_op jit(solution)/shard_map/ppermute | solution.py:14
  896.6 1.1 copy-start.10
  896.6 1.2 copy-start.14
  896.6 1.2 copy-start.17
  896.7 1.2 copy-start.18
  899.7 79.7 %collective-permute-start.11 = (f32[6,1536]{1,0:T(8,128)S(1)}, f32[6,1536]{1,0:T(8,128)S(1)}, u32[]{:S(2)}, u32[]{:S(2)}) collective-permute-start(f32[6,1536]{1,0:T(8,128)S(1)} %slice.294), channel_id=1, source_target_pairs={{1,0},{2,1},{3,2},{4,3},{5,4},{6,5},{7,6},{8,7},{9,8},{10,9},{11,1... | collective-permute-start | bytes 110600 | tf_op jit(solution)/shard_map/ppermute | solution.py:20
Sparse Core Ops, SparseCore 0:
  899.0 27.2 all-gather.2
